TPU v7x, 32 devices: a whole 2x2x4 slice. The times are simulated.
32 devices in a mesh: grid: 8 (over y, x, core), pt: 4 (over z).
Axes of the slice: x: 2, y: 2, z: 4, core: 2. Of those that a mesh axis runs over, the one named last changes fastest.
Arguments:
- orbitals: bfloat16 [2048, 4096], P('grid'), may hold values from -0.875 to 0.875
- point_index: int32 [2048], P('pt'), may hold values from 0 to 4095, as said below
- factor_panels: float32 [2048, 1024], P('pt'), as said below
Outputs:
- solved: float32 [4096, 2048], P('grid', 'pt')
Inputs may be any that keep to these rules, and one draw needn't show every extreme that they name: `point_index`: all entries are different; 0 and 4095 are always among them. `factor_panels`: lower triangular in its global row and column indices, diagonal between 1.5 and 3.
All inputs are finite; a program needn't handle non-finite values.
Results may differ from a plain program's by a relative error of at most 0.0018.
Values may be sent and summed in bfloat16 or wider, within the bound.
A program may use at most 64 MiB of HBM per device.

v0:
```python
import jax
import jax.numpy as jnp
from jax import lax
from jax.sharding import PartitionSpec as P


def spread(x, axis, root):
    mine = lax.axis_index(axis) == root
    return lax.psum(jnp.where(mine, x, jnp.zeros_like(x)), axis)


def solve_panel(factor, targets):
    return lax.linalg.triangular_solve(
        factor, targets, left_side=False, lower=True, transpose_a=True
    )


def apply_factor(panel_round, factor):
    upper_part = factor.astype(jnp.bfloat16)
    lower_part = (factor - upper_part.astype(jnp.float32)).astype(jnp.bfloat16)
    dims = (((1,), (1,)), ((), ()))
    high_term = lax.dot_general(panel_round, upper_part, dims, preferred_element_type=jnp.float32)
    low_term = lax.dot_general(panel_round, lower_part, dims, preferred_element_type=jnp.float32)
    return high_term + low_term


def on_device(orbitals, point_index, factor_panels):
    own_bands, grid_rows = orbitals.shape
    grid_count = lax.axis_size("grid")
    rows_here = grid_rows // grid_count
    panel_cols = point_index.shape[0]
    at_points = jnp.take(orbitals, point_index, axis=1)
    point_orbs = lax.all_gather(at_points, "grid", axis=0, tiled=True)
    blocked = orbitals.reshape(own_bands, grid_count, rows_here)
    inner_sums = lax.dot_general(
        lax.all_to_all(blocked, "grid", split_axis=1, concat_axis=0, tiled=True)[:, 0, :],
        point_orbs,
        (((0,), (0,)), ((), ())),
        preferred_element_type=jnp.float32,
    )
    products = inner_sums * inner_sums
    rank_pt = lax.axis_index("pt")
    factor_first = factor_panels[:, 0:panel_cols]
    factor_second = factor_panels[:, panel_cols : 2 * panel_cols]
    first_solved = lax.cond(
        rank_pt == 0, lambda: solve_panel(factor_first, products), lambda: jnp.zeros_like(products)
    )
    first_round = spread(first_solved.astype(jnp.bfloat16), "pt", 0)
    left_over = lax.cond(
        rank_pt > 0, lambda: products - apply_factor(first_round, factor_first), lambda: products
    )
    second_solved = lax.cond(
        rank_pt == 1,
        lambda: solve_panel(factor_second, left_over),
        lambda: jnp.zeros_like(left_over),
    )
    second_round = spread(second_solved.astype(jnp.bfloat16), "pt", 1)
    trailing = lax.cond(
        rank_pt > 1,
        lambda: left_over - apply_factor(second_round, factor_second),
        lambda: left_over,
    )
    return jnp.where(rank_pt == 0, first_solved, jnp.where(rank_pt == 1, second_solved, trailing))


def solution(mesh):
    in_specs = (P("grid", None), P("pt"), P("pt", None))
    out_specs = P("grid", "pt")
    return jax.shard_map(
        on_device, mesh=mesh, in_specs=in_specs, out_specs=out_specs, check_vma=False
    )
```

profile of v0, /device:TPU:24, one launch (start us, length us, event | category | flops | bytes accessed | tf_op | source)
XLA Modules:
  0.0 290.6 jit_solution(4851775570383524236)
XLA Ops:
  7.9 4.1 %copy.26 = bf16[256,4096]{0,1:T(8,128)(2,1)} copy(bf16[256,4096]{1,0:T(8,128)(2,1)} %param.13) | data formatting | bytes 4194304 | tf_op args[0]
  12.0 3.4 %gather_fusion = bf16[512,256]{1,0:T(8,128)(2,1)S(1)} fusion(bf16[256,4096]{0,1:T(8,128)(2,1)} %copy.26, s32[1024]{0:T(1024)S(1)} %pad_clamp_fusion), kind=kCustom, calls=%fused_computation | custom fusion | bytes 526336 | tf_op jit(solution)/shard_map/jit(_take)/gather | solution.py:32
  15.4 0.8 select_bitcast_fusion
  16.3 4.4 %all-to-all-start = ((bf16[256,8,512]{0,2,1:T(8,128)(2,1)}), bf16[256,8,512]{0,2,1:T(8,128)(2,1)}, u32[]{:S(2)}, u32[]{:S(2)}) async-start(bf16[256,8,512]{0,2,1:T(8,128)(2,1)} %bitcast.13), calls=%async_computation | async-start | bytes 4194304 | tf_op jit(solution)/shard_map/all_to_all | solution.py:36
  20.7 1.7 fusion.53
  22.4 31.9 %all-to-all-done = bf16[256,8,512]{0,2,1:T(8,128)(2,1)} async-done(((bf16[256,8,512]{0,2,1:T(8,128)(2,1)}), bf16[256,8,512]{0,2,1:T(8,128)(2,1)}, u32[]{:S(2)}, u32[]{:S(2)}) %all-to-all-start) | async-done | bytes 2097184 | tf_op jit(solution)/shard_map/all_to_all | solution.py:36
  54.4 4.0 %copy.28 = bf16[8,256,1,512]{3,1,0,2:T(8,128)(2,1)} copy(bf16[8,256,1,512]{1,3,0,2:T(8,128)(2,1)} %bitcast.15) | data formatting | bytes 4194304 | tf_op jit(solution)/shard_map/all_to_all | solution.py:36
  58.3 3.5 %fusion.50 = f32[512,512]{0,1:T(8,128)S(1)} fusion(bf16[2048,512]{0,1:T(8,128)(2,1)} %all-gather.2.cloned.1.call-done, bf16[2048,512]{1,0:T(8,128)(2,1)} %bitcast.89), kind=kOutput, calls=%fused_computation.80 | convolution fusion | flops 1074003968 | bytes 5242880 | tf_op jit(solution)/shard_map/dot_general | solution.py:35
  61.8 1.9 conditional.4
  61.8 1.1 broadcast.26.clone
  63.7 0.9 broadcast_select_fusion.1
  64.7 103.3 %all-reduce.3.cloned.1.call-done = bf16[512,512]{1,0:T(8,128)(2,1)} async-done(((bf16[512,512]{1,0:T(8,128)(2,1)}), bf16[512,512]{1,0:T(8,128)(2,1)}) %all-reduce.3.cloned.1.call-update) | async-done | bytes 524304 | tf_op jit(solution)/shard_map/psum | solution.py:9
  167.9 6.0 %conditional.5 = (f32[512,512]{1,0:T(8,128)S(1)}) conditional(s32[]{:T(128)} %convert_element_type.44, (f32[512,512]{0,1:T(8,128)S(1)}) %tuple.61, (f32[512,512]{1,0:T(8,128)S(1)}, bf16[512,512]{1,0:T(8,128)(2,1)}, f32[512,512]{0,1:T(8,128)S(1)}) %tuple.41), branch_computations={%region_3.5_spmd, %region_4.6_spmd} | conditional | flops 538705920 | bytes 9437192 | solution.py:49
  167.9 2.5 fusion.3
  170.4 1.3 copy.32
  171.8 2.2 fusion.1
  173.9 2.0 conditional.6
  174.0 1.1 broadcast.31.clone
  175.1 0.8 broadcast.32.clone
  175.9 0.8 broadcast_select_fusion
  176.8 103.7 %all-reduce.5.cloned.1.call-done = bf16[512,512]{1,0:T(8,128)(2,1)} async-done(((bf16[512,512]{1,0:T(8,128)(2,1)}), bf16[512,512]{1,0:T(8,128)(2,1)}) %all-reduce.5.cloned.1.call-update) | async-done | bytes 524304 | tf_op jit(solution)/shard_map/psum | solution.py:9
  280.5 2.2 conditional.7
  280.5 1.6 fusion.8
  282.7 1.3 select_select_fusion
  (14 shorter events, 2.9 us)
Async XLA Ops:
  6.5 51.8 %all-gather.2.cloned.1.call-start = ((), (), s32[]{:S(2)}) async-start(), calls=%async_computation.1 | async-start | bytes 2359296 | tf_op jit(solution)/shard_map/all_gather | solution.py:33
  16.3 38.1 %all-to-all-start = ((bf16[256,8,512]{0,2,1:T(8,128)(2,1)}), bf16[256,8,512]{0,2,1:T(8,128)(2,1)}, u32[]{:S(2)}, u32[]{:S(2)}) async-start(bf16[256,8,512]{0,2,1:T(8,128)(2,1)} %bitcast.13), calls=%async_computation | async-start | bytes 4194304 | tf_op jit(solution)/shard_map/all_to_all | solution.py:36
  20.7 147.3 %all-reduce.3.cloned.1.call-start = ((), (), s32[]{:S(2)}) async-start(), calls=%async_computation.2 | async-start | bytes 1048576 | tf_op jit(solution)/shard_map/psum | solution.py:9
  64.6 215.9 %all-reduce.5.cloned.1.call-start = ((), (), s32[]{:S(2)}) async-start(), calls=%async_computation.3 | async-start | bytes 1048576 | tf_op jit(solution)/shard_map/psum | solution.py:9
  280.5 1.6 copy-start.6
Sparse Core Ops, SparseCore 0:
  16.4 41.0 all-gather.1
  64.7 103.1 all-reduce.2
  176.9 103.5 all-reduce.4
where the time goes:
time: 293 us; the launch traced here: 291 us
  waiting for transfers between devices  239 us (82%)
  local copies, waits for them, and re-layouts  18.4 us (6%)
  between operations  13.2 us (5%)
  matrix products  10.3 us (4%)
  other arithmetic  5.24 us (2%)
  starting transfers between devices  4.45 us (2%)
    psum x2, waiting for transfers between devices, spread(): return lax.psum(jnp.where(mine, x, jnp.zeros_like(x)), axis)  207 us
    all_to_all x1, waiting for transfers between devices, on_device(): lax.all_to_all(blocked, 'grid', split_axis=1, concat_axis=0, tiled=True)  31.9 us
  transfers between devices with their start and end apart: 4, of which 3 were waited for; matrix products, arithmetic and copies ran while one was open for 2% of the time, Pallas kernels for 0%

commit v1 on v0

v1 whole, which is shorter than its diff:
```python
import functools
import jax
import jax.numpy as jnp
from jax import lax
from jax.experimental import pallas as pl
from jax.experimental.pallas import tpu as pltpu
from jax.sharding import PartitionSpec as P

MESH = pl.DeviceIdType.MESH
F32, BF16 = jnp.float32, jnp.bfloat16
LANES = 128


def split(value):
    high = value.astype(BF16)
    return high, (value - high.astype(F32)).astype(BF16)


def dot(a, b):
    return jnp.dot(a, b, preferred_element_type=F32)


def exact_dot(a, b):
    return jnp.dot(a, b, preferred_element_type=F32, precision=lax.Precision.HIGHEST)


def invert_lower(low, inv):
    size = low.shape[0]
    blocks = size // LANES
    row = lax.broadcasted_iota(jnp.int32, (LANES, LANES), 0)
    col = lax.broadcasted_iota(jnp.int32, (LANES, LANES), 1)
    tiles, parts = [], []
    for i in range(blocks):
        at = slice(i * LANES, (i + 1) * LANES)
        tile = low[at, at]
        tiles.append(tile)
        parts.append(jnp.where(row == col, 1.0 / jnp.where(row == col, tile, 1.0), 0.0))
    half = 1
    level = 0
    while half < LANES:
        rb, cb = row >> level, col >> level
        mask = ((rb >> 1) == (cb >> 1)) & (rb > cb)
        mids = [exact_dot(jnp.where(mask, tiles[i], 0.0), parts[i]) for i in range(blocks)]
        parts = [parts[i] - exact_dot(parts[i], mids[i]) for i in range(blocks)]
        half *= 2
        level += 1
    inv[...] = jnp.zeros_like(inv)
    for i in range(blocks):
        at = slice(i * LANES, (i + 1) * LANES)
        inv[at, at] = parts[i]
    width = LANES
    while width < size:
        for start in range(0, size, 2 * width):
            top = slice(start, start + width)
            bottom = slice(start + width, start + 2 * width)
            mid = exact_dot(low[bottom, top], inv[top, top])
            inv[bottom, top] = -exact_dot(inv[bottom, bottom], mid)
        width *= 2


def kernel(
    grid_count, pt_count, index_ref, orb, fac, out,
    orb_v, fac_v, rows, points, gathered, low, inv, a_high, a_low, b_high, b_low, firsts, seconds,
    load_sem, own_sem, row_send, row_recv, point_send, point_recv, pass_send,
    first_send, first_recv, second_send, second_recv,
):
    me = lax.axis_index("grid")
    rank = lax.axis_index("pt")
    own_bands, grid_rows = orb.shape
    chunks = rows.shape[0]
    panel = index_ref.shape[1]
    rows_here = chunks * LANES
    partner = me + 1 - 2 * lax.rem(me, 2)
    pairs = grid_count // 2

    def own_block(g):
        return pl.ds(pl.multiple_of(g * own_bands, own_bands), own_bands)

    load_orb = pltpu.make_async_copy(orb, orb_v, load_sem.at[0])
    load_fac = pltpu.make_async_copy(fac, fac_v, load_sem.at[1])
    load_orb.start()

    barrier = pltpu.get_barrier_semaphore()

    @pl.loop(1, grid_count)
    def _(k):
        other = lax.rem(me + k, grid_count)
        pl.semaphore_signal(barrier, inc=1, device_id=(other, rank), device_id_type=MESH)

    @pl.when(rank > 0)
    def _():
        pl.semaphore_signal(barrier, inc=1, device_id=(me, rank - 1), device_id_type=MESH)

    @pl.when(rank < pt_count - 1)
    def _():
        pl.semaphore_signal(barrier, inc=1, device_id=(me, rank + 1), device_id_type=MESH)

    at_end = (rank == 0) | (rank == pt_count - 1)

    @pl.when(at_end)
    def _():
        pl.semaphore_wait(barrier, grid_count)

    @pl.when(jnp.logical_not(at_end))
    def _():
        pl.semaphore_wait(barrier, grid_count + 1)

    def row_cols(g, c):
        return pl.ds(pl.multiple_of(g * rows_here + c * LANES, LANES), LANES)

    def send_rows(c):
        @pl.loop(1, grid_count)
        def _(k):
            other = lax.rem(me + k, grid_count)
            pltpu.make_async_remote_copy(
                src_ref=orb.at[:, row_cols(other, c)],
                dst_ref=rows.at[c, own_block(me), :],
                send_sem=row_send.at[c],
                recv_sem=row_recv.at[c],
                device_id=(other, rank),
                device_id_type=MESH,
            ).start()

    send_rows(0)
    owns = []
    for c in range(chunks):
        own = pltpu.make_async_copy(orb.at[:, row_cols(me, c)], rows.at[c, own_block(me), :], own_sem.at[c])
        own.start()
        owns.append(own)
    load_fac.start()
    load_orb.wait()

    depth = min(1024, grid_rows)
    gathered[...] = jnp.zeros_like(gathered)

    @pl.loop(0, grid_rows // depth)
    def _(s):
        ids = lax.broadcasted_iota(jnp.int32, (depth, panel), 0) + s * depth
        hot = jnp.where(ids == index_ref[...], 1.0, 0.0).astype(BF16)
        gathered[...] += dot(orb_v[:, pl.ds(pl.multiple_of(s * depth, depth), depth)], hot)

    points[own_block(me), :] = gathered[...].astype(BF16)

    def point_copy(g, target, send_sem):
        return pltpu.make_async_remote_copy(
            src_ref=points.at[own_block(g), :],
            dst_ref=points.at[own_block(g), :],
            send_sem=send_sem,
            recv_sem=point_recv.at[g],
            device_id=(target, rank),
            device_id_type=MESH,
        )

    @pl.loop(1, pairs)
    def _(k):
        point_copy(me, lax.rem(me + 2 * k, grid_count), point_send.at[k]).start()

    point_copy(me, partner, pass_send.at[0]).start()
    for c in range(1, chunks):
        send_rows(c)

    load_fac.wait()

    @pl.when(rank < 2)
    def _():
        start = pl.multiple_of(rank * panel, panel)
        low[...] = fac_v[:, pl.ds(start, panel)]
        invert_lower(low, inv)

    @pl.when(rank > 0)
    def _():
        a_high[...], a_low[...] = split(fac_v[:, 0:panel].T)

    @pl.when(rank == 0)
    def _():
        a_high[...], a_low[...] = split(inv[...].T)

    @pl.when(rank > 1)
    def _():
        b_high[...], b_low[...] = split(fac_v[:, panel : 2 * panel].T)

    @pl.when(rank == 1)
    def _():
        b_high[...], b_low[...] = split(inv[...].T)

    @pl.loop(1, pairs)
    def _(k):
        source = lax.rem(me + 2 * (pairs - k), grid_count)
        point_copy(source, me, point_send.at[k]).wait_recv()
        point_copy(source, partner, pass_send.at[k]).start()

    @pl.loop(0, pairs)
    def _(k):
        source = lax.rem(partner + 2 * k, grid_count)
        point_copy(source, me, pass_send.at[k]).wait_recv()

    def chain(buf, c, send_sem, recv_sem):
        return pltpu.make_async_remote_copy(
            src_ref=buf.at[c],
            dst_ref=buf.at[c],
            send_sem=send_sem.at[c],
            recv_sem=recv_sem.at[c],
            device_id=(me, rank + 1),
            device_id_type=MESH,
        )

    def solve(value, high, low_part):
        value_high, value_low = split(value)
        return dot(value_high, high[...]) + (dot(value_high, low_part[...]) + dot(value_low, high[...]))

    def apply(value, high, low_part):
        return dot(value, high[...]) + dot(value, low_part[...])

    others = pl.ds(0, (grid_count - 1) * own_bands)

    @pl.loop(0, chunks)
    def _(c):
        pltpu.make_async_copy(rows.at[c, others, :], rows.at[c, others, :], row_recv.at[c]).wait()
        pltpu.make_async_copy(
            orb.at[:, pl.ds(0, LANES)], rows.at[c, own_block(me), :], own_sem.at[c]
        ).wait()
        sums = lax.dot_general(
            rows[c], points[...], (((0,), (0,)), ((), ())), preferred_element_type=F32
        )
        here = pl.ds(pl.multiple_of(c * LANES, LANES), LANES)
        out[here, :] = sums * sums

        @pl.when(rank == 0)
        def _():
            first = solve(out[here, :], a_high, a_low)
            out[here, :] = first
            firsts[c] = first.astype(BF16)

        @pl.when(rank > 0)
        def _():
            chain(firsts, c, first_send, first_recv).wait_recv()

        @pl.when(rank < pt_count - 1)
        def _():
            chain(firsts, c, first_send, first_recv).start()

        @pl.when(rank > 0)
        def _():
            out[here, :] -= apply(firsts[c], a_high, a_low)

        @pl.when(rank == 1)
        def _():
            second = solve(out[here, :], b_high, b_low)
            out[here, :] = second
            seconds[c] = second.astype(BF16)

        @pl.when(rank > 1)
        def _():
            chain(seconds, c, second_send, second_recv).wait_recv()

        @pl.when((rank > 0) & (rank < pt_count - 1))
        def _():
            chain(seconds, c, second_send, second_recv).start()

        @pl.when(rank > 1)
        def _():
            out[here, :] -= apply(seconds[c], b_high, b_low)

    @pl.loop(0, chunks)
    def _(c):
        pltpu.make_async_copy(rows.at[c, others, :], rows.at[c, others, :], row_send.at[c]).wait()

        @pl.when(rank < pt_count - 1)
        def _():
            chain(firsts, c, first_send, first_recv).wait_send()

        @pl.when((rank > 0) & (rank < pt_count - 1))
        def _():
            chain(seconds, c, second_send, second_recv).wait_send()

    @pl.loop(1, pairs)
    def _(k):
        point_copy(me, partner, point_send.at[k]).wait_send()

    @pl.loop(0, pairs)
    def _(k):
        point_copy(me, partner, pass_send.at[k]).wait_send()


def on_device(grid_count, pt_count, orbitals, point_index, factor_panels):
    own_bands, grid_rows = orbitals.shape
    rows_here = grid_rows // grid_count
    panel = point_index.shape[0]
    chunks = rows_here // LANES
    bands = own_bands * grid_count
    vmem = pl.BlockSpec(memory_space=pltpu.VMEM)
    hbm = pl.BlockSpec(memory_space=pl.ANY)
    dma = pltpu.SemaphoreType.DMA
    return pl.pallas_call(
        functools.partial(kernel, grid_count, pt_count),
        out_shape=jax.ShapeDtypeStruct((rows_here, panel), F32),
        in_specs=[vmem, hbm, hbm],
        out_specs=vmem,
        scratch_shapes=[
            pltpu.VMEM((own_bands, grid_rows), BF16),
            pltpu.VMEM(factor_panels.shape, F32),
            pltpu.VMEM((chunks, bands, LANES), BF16),
            pltpu.VMEM((bands, panel), BF16),
            pltpu.VMEM((own_bands, panel), F32),
            pltpu.VMEM((panel, panel), F32),
            pltpu.VMEM((panel, panel), F32),
            pltpu.VMEM((panel, panel), BF16),
            pltpu.VMEM((panel, panel), BF16),
            pltpu.VMEM((panel, panel), BF16),
            pltpu.VMEM((panel, panel), BF16),
            pltpu.VMEM((chunks, LANES, panel), BF16),
            pltpu.VMEM((chunks, LANES, panel), BF16),
            dma((2,)),
            dma((chunks,)),
            dma((chunks,)),
            dma((chunks,)),
            dma((grid_count // 2,)),
            dma((grid_count,)),
            dma((grid_count // 2,)),
            dma((chunks,)),
            dma((chunks,)),
            dma((chunks,)),
            dma((chunks,)),
        ],
        compiler_params=pltpu.CompilerParams(
            collective_id=0, has_side_effects=True, vmem_limit_bytes=56 * 1024 * 1024
        ),
    )(point_index.reshape(1, panel), orbitals, factor_panels)


def solution(mesh):
    in_specs = (P("grid", None), P("pt"), P("pt", None))
    out_specs = P("grid", "pt")
    body = functools.partial(on_device, mesh.shape["grid"], mesh.shape["pt"])
    return jax.shard_map(
        body, mesh=mesh, in_specs=in_specs, out_specs=out_specs, check_vma=False
    )
```

time: 293 us -> 61.2 us (0.21)
  waiting for transfers between devices: 239 us -> 0 us
  Pallas kernels: 0 us -> 58.2 us
  local copies, waits for them, and re-layouts: 18.4 us -> 2.26 us
  between operations: 13.2 us -> 0.01 us
  matrix products: 10.3 us -> 0 us
  other arithmetic: 5.24 us -> 0 us
  starting transfers between devices: 4.45 us -> 0 us
    psum x2 -> x0, waiting for transfers between devices: 207 us -> none  [spread(): return lax.psum(jnp.where(mine, x, jnp.zeros_like(x)), axis)]
    pallas_call x0 -> x1, Pallas kernels: none -> 58.2 us  [on_device(): pl.pallas_call(functools.partial(kernel, grid_count, pt_count), out_shape...]
    all_to_all x1 -> x0, waiting for transfers between devices: 31.9 us -> none  [on_device(): lax.all_to_all(blocked, 'grid', split_axis=1, concat_axis=0, tiled=True)]
    dot_general x5 -> x0, matrix products: 10.3 us -> none  [the longest x2 4.06 us: apply_factor(): lax.dot_general(panel_round, upper_part, dims, preferred_element_type=jnp...]
    another operation x5 -> x0, local copies, waits for them, and re-layouts: 5.26 us -> none
    select_n x5 -> x0, other arithmetic: 4.54 us -> none  [the longest x2 1.68 us: spread(): return lax.psum(jnp.where(mine, x, jnp.zeros_like(x)), axis)]
    all_to_all x1 -> x0, starting transfers between devices: 4.36 us -> none  [on_device(): lax.all_to_all(blocked, 'grid', split_axis=1, concat_axis=0, tiled=True)]
    all_to_all x1 -> x0, local copies, waits for them, and re-layouts: 3.96 us -> none  [on_device(): lax.all_to_all(blocked, 'grid', split_axis=1, concat_axis=0, tiled=True)]
  transfers between devices with their start and end apart: 4 -> 0, of which waited for: 3 -> 0; matrix products, arithmetic and copies ran while one was open for 2% -> 0% of each run, Pallas kernels for 0% -> 0%
where the time goes in v1:
time: 61.2 us; the launch traced here: 60.5 us
  Pallas kernels  58.2 us (95%)
  local copies, waits for them, and re-layouts  2.26 us (4%)
    pallas_call x1, Pallas kernels, on_device(): pl.pallas_call(functools.partial(kernel, grid_count, pt_count), out_shape...  58.2 us
    unnamed x1, local copies, waits for them, and re-layouts  2.26 us

profile of v1, /device:TPU:24, one launch (start us, length us, event | category | flops | bytes accessed | tf_op | source)
XLA Modules:
  0.0 60.5 jit_solution(10387163893754559312)
XLA Ops:
  0.0 58.2 %shard_map.37 = f32[512,512]{1,0:T(8,128)} custom-call(s32[1,512]{1,0:T(1,128)} %bitcast.1, bf16[256,4096]{1,0:T(8,128)(2,1)} %orb.1, f32[512,1024]{1,0:T(8,128)} %fac.1), custom_call_target="tpu_custom_call" | custom-call | tf_op jit(solution)/shard_map/pallas_call | solution.py:294
  58.2 2.3 %copy.5 = f32[512,512]{1,0:T(8,128)} copy(f32[512,512]{1,0:T(8,128)} %shard_map.37) | data formatting | bytes 2097152

commit v2 on v1

--- a/solution.py
+++ b/solution.py
@@ -9,6 +9,7 @@
 MESH = pl.DeviceIdType.MESH
 F32, BF16 = jnp.float32, jnp.bfloat16
 LANES = 128
+PIECE = 64
 
 
 def split(value):
@@ -61,20 +62,32 @@
 def kernel(
     grid_count, pt_count, index_ref, orb, fac, out,
     orb_v, fac_v, rows, points, gathered, low, inv, a_high, a_low, b_high, b_low, firsts, seconds,
-    load_sem, own_sem, row_send, row_recv, point_send, point_recv, pass_send,
+    load_sem, own_sem, row_send, row_recv, sibling_recv, late_send, help_send, help_recv,
+    point_send, point_recv, pass_send,
     first_send, first_recv, second_send, second_recv,
 ):
     me = lax.axis_index("grid")
     rank = lax.axis_index("pt")
     own_bands, grid_rows = orb.shape
+    half_bands = own_bands // 2
     chunks = rows.shape[0]
     panel = index_ref.shape[1]
     rows_here = chunks * LANES
     partner = me + 1 - 2 * lax.rem(me, 2)
+    chip = me - lax.rem(me, 2)
     pairs = grid_count // 2
-
-    def own_block(g):
-        return pl.ds(pl.multiple_of(g * own_bands, own_bands), own_bands)
+    far = grid_count - 2
+    last = pt_count - 1
+    mine = lax.rem(pt_count - rank, 2)
+
+    def block(g):
+        return pl.ds(pl.multiple_of(g * half_bands, half_bands), half_bands)
+
+    def half_of(h):
+        return pl.ds(pl.multiple_of(h * half_bands, half_bands), half_bands)
+
+    def far_one(i):
+        return lax.rem(chip + 2 + i, grid_count)
 
     load_orb = pltpu.make_async_copy(orb, orb_v, load_sem.at[0])
     load_fac = pltpu.make_async_copy(fac, fac_v, load_sem.at[1])
@@ -91,11 +104,11 @@
     def _():
         pl.semaphore_signal(barrier, inc=1, device_id=(me, rank - 1), device_id_type=MESH)
 
-    @pl.when(rank < pt_count - 1)
+    @pl.when(rank < last)
     def _():
         pl.semaphore_signal(barrier, inc=1, device_id=(me, rank + 1), device_id_type=MESH)
 
-    at_end = (rank == 0) | (rank == pt_count - 1)
+    at_end = (rank == 0) | (rank == last)
 
     @pl.when(at_end)
     def _():
@@ -108,25 +121,30 @@
     def row_cols(g, c):
         return pl.ds(pl.multiple_of(g * rows_here + c * LANES, LANES), LANES)
 
+    def row_copy(c, h, target, send_sem, recv_sem):
+        return pltpu.make_async_remote_copy(
+            src_ref=orb.at[half_of(h), row_cols(target, c)],
+            dst_ref=rows.at[c, h, block(me), :],
+            send_sem=send_sem.at[c],
+            recv_sem=recv_sem.at[c],
+            device_id=(target, rank),
+            device_id_type=MESH,
+        )
+
     def send_rows(c):
-        @pl.loop(1, grid_count)
-        def _(k):
-            other = lax.rem(me + k, grid_count)
-            pltpu.make_async_remote_copy(
-                src_ref=orb.at[:, row_cols(other, c)],
-                dst_ref=rows.at[c, own_block(me), :],
-                send_sem=row_send.at[c],
-                recv_sem=row_recv.at[c],
-                device_id=(other, rank),
-                device_id_type=MESH,
+        @pl.loop(0, far)
+        def _(i):
+            row_copy(c, mine, far_one(i), row_send, row_recv).start()
+
+        row_copy(c, 0, partner, row_send, sibling_recv).start()
+        row_copy(c, 1, partner, row_send, sibling_recv).start()
+
+    send_rows(0)
+    for c in range(chunks):
+        for h in range(2):
+            pltpu.make_async_copy(
+                orb.at[half_of(h), row_cols(me, c)], rows.at[c, h, block(me), :], own_sem.at[c]
             ).start()
-
-    send_rows(0)
-    owns = []
-    for c in range(chunks):
-        own = pltpu.make_async_copy(orb.at[:, row_cols(me, c)], rows.at[c, own_block(me), :], own_sem.at[c])
-        own.start()
-        owns.append(own)
     load_fac.start()
     load_orb.wait()
 
@@ -139,12 +157,13 @@
         hot = jnp.where(ids == index_ref[...], 1.0, 0.0).astype(BF16)
         gathered[...] += dot(orb_v[:, pl.ds(pl.multiple_of(s * depth, depth), depth)], hot)
 
-    points[own_block(me), :] = gathered[...].astype(BF16)
+    points[0, block(me), :] = gathered[0:half_bands, :].astype(BF16)
+    points[1, block(me), :] = gathered[half_bands:own_bands, :].astype(BF16)
 
     def point_copy(g, target, send_sem):
         return pltpu.make_async_remote_copy(
-            src_ref=points.at[own_block(g), :],
-            dst_ref=points.at[own_block(g), :],
+            src_ref=points.at[:, block(g), :],
+            dst_ref=points.at[:, block(g), :],
             send_sem=send_sem,
             recv_sem=point_recv.at[g],
             device_id=(target, rank),
@@ -159,6 +178,39 @@
     for c in range(1, chunks):
         send_rows(c)
 
+    @pl.when(rank == last)
+    def _():
+        for c in range(chunks):
+
+            @pl.loop(0, far)
+            def _(i):
+                row_copy(c, 1 - mine, far_one(i), late_send, help_recv).start()
+
+    def settle(c, count, sem):
+        part = rows.at[c, 0, pl.ds(0, count), :]
+        pltpu.make_async_copy(part, part, sem.at[c]).wait()
+
+    def forward(c):
+        settle(c, far * half_bands, row_recv)
+
+        @pl.when(rank > 0)
+        def _():
+            @pl.loop(0, far)
+            def _(i):
+                part = rows.at[c, mine, block(far_one(i)), :]
+                pltpu.make_async_remote_copy(
+                    src_ref=part,
+                    dst_ref=part,
+                    send_sem=help_send.at[c],
+                    recv_sem=help_recv.at[c],
+                    device_id=(me, rank - 1),
+                    device_id_type=MESH,
+                ).start()
+
+    @pl.when(rank > 0)
+    def _():
+        forward(0)
+
     load_fac.wait()
 
     @pl.when(rank < 2)
@@ -189,17 +241,23 @@
         point_copy(source, me, point_send.at[k]).wait_recv()
         point_copy(source, partner, pass_send.at[k]).start()
 
+    for c in range(1, chunks):
+
+        @pl.when(rank > c)
+        def _():
+            forward(c)
+
     @pl.loop(0, pairs)
     def _(k):
         source = lax.rem(partner + 2 * k, grid_count)
         point_copy(source, me, pass_send.at[k]).wait_recv()
 
-    def chain(buf, c, send_sem, recv_sem):
+    def chain(buf, p, send_sem, recv_sem):
         return pltpu.make_async_remote_copy(
-            src_ref=buf.at[c],
-            dst_ref=buf.at[c],
-            send_sem=send_sem.at[c],
-            recv_sem=recv_sem.at[c],
+            src_ref=buf.at[p],
+            dst_ref=buf.at[p],
+            send_sem=send_sem.at[p],
+            recv_sem=recv_sem.at[p],
             device_id=(me, rank + 1),
             device_id_type=MESH,
         )
@@ -211,67 +269,84 @@
     def apply(value, high, low_part):
         return dot(value, high[...]) + dot(value, low_part[...])
 
-    others = pl.ds(0, (grid_count - 1) * own_bands)
+    piece = firsts.shape[1]
+    pieces = LANES // piece
 
     @pl.loop(0, chunks)
     def _(c):
-        pltpu.make_async_copy(rows.at[c, others, :], rows.at[c, others, :], row_recv.at[c]).wait()
-        pltpu.make_async_copy(
-            orb.at[:, pl.ds(0, LANES)], rows.at[c, own_block(me), :], own_sem.at[c]
-        ).wait()
-        sums = lax.dot_general(
-            rows[c], points[...], (((0,), (0,)), ((), ())), preferred_element_type=F32
-        )
-        here = pl.ds(pl.multiple_of(c * LANES, LANES), LANES)
-        out[here, :] = sums * sums
-
-        @pl.when(rank == 0)
-        def _():
-            first = solve(out[here, :], a_high, a_low)
-            out[here, :] = first
-            firsts[c] = first.astype(BF16)
-
-        @pl.when(rank > 0)
-        def _():
-            chain(firsts, c, first_send, first_recv).wait_recv()
-
-        @pl.when(rank < pt_count - 1)
-        def _():
-            chain(firsts, c, first_send, first_recv).start()
-
-        @pl.when(rank > 0)
-        def _():
-            out[here, :] -= apply(firsts[c], a_high, a_low)
-
-        @pl.when(rank == 1)
-        def _():
-            second = solve(out[here, :], b_high, b_low)
-            out[here, :] = second
-            seconds[c] = second.astype(BF16)
-
-        @pl.when(rank > 1)
-        def _():
-            chain(seconds, c, second_send, second_recv).wait_recv()
-
-        @pl.when((rank > 0) & (rank < pt_count - 1))
-        def _():
-            chain(seconds, c, second_send, second_recv).start()
-
-        @pl.when(rank > 1)
-        def _():
-            out[here, :] -= apply(seconds[c], b_high, b_low)
+        @pl.when(c + rank < chunks)
+        def _():
+            forward(c + rank)
+
+        settle(c, own_bands, own_sem)
+        settle(c, own_bands, sibling_recv)
+        settle(c, far * half_bands, help_recv)
+        over_bands = (((0,), (0,)), ((), ()))
+        sums = lax.dot_general(rows[c, 0], points[0], over_bands, preferred_element_type=F32)
+        sums += lax.dot_general(rows[c, 1], points[1], over_bands, preferred_element_type=F32)
+        out[pl.ds(pl.multiple_of(c * LANES, LANES), LANES), :] = sums * sums
+
+        @pl.loop(c * pieces, (c + 1) * pieces)
+        def _(p):
+            here = pl.ds(pl.multiple_of(p * piece, piece), piece)
+
+            @pl.when(rank == 0)
+            def _():
+                first = solve(out[here, :], a_high, a_low)
+                out[here, :] = first
+                firsts[p] = first.astype(BF16)
+
+            @pl.when(rank > 0)
+            def _():
+                chain(firsts, p, first_send, first_recv).wait_recv()
+
+            @pl.when(rank < last)
+            def _():
+                chain(firsts, p, first_send, first_recv).start()
+
+            @pl.when(rank > 0)
+            def _():
+                out[here, :] -= apply(firsts[p], a_high, a_low)
+
+            @pl.when(rank == 1)
+            def _():
+                second = solve(out[here, :], b_high, b_low)
+                out[here, :] = second
+                seconds[p] = second.astype(BF16)
+
+            @pl.when(rank > 1)
+            def _():
+                chain(seconds, p, second_send, second_recv).wait_recv()
+
+            @pl.when((rank > 0) & (rank < last))
+            def _():
+                chain(seconds, p, second_send, second_recv).start()
+
+            @pl.when(rank > 1)
+            def _():
+                out[here, :] -= apply(seconds[p], b_high, b_low)
 
     @pl.loop(0, chunks)
     def _(c):
-        pltpu.make_async_copy(rows.at[c, others, :], rows.at[c, others, :], row_send.at[c]).wait()
-
-        @pl.when(rank < pt_count - 1)
-        def _():
-            chain(firsts, c, first_send, first_recv).wait_send()
-
-        @pl.when((rank > 0) & (rank < pt_count - 1))
-        def _():
-            chain(seconds, c, second_send, second_recv).wait_send()
+        settle(c, grid_count * half_bands, row_send)
+
+        @pl.when(rank == last)
+        def _():
+            settle(c, far * half_bands, late_send)
+
+        @pl.when(rank > 0)
+        def _():
+            settle(c, far * half_bands, help_send)
+
+    @pl.loop(0, chunks * pieces)
+    def _(p):
+        @pl.when(rank < last)
+        def _():
+            chain(firsts, p, first_send, first_recv).wait_send()
+
+        @pl.when((rank > 0) & (rank < last))
+        def _():
+            chain(seconds, p, second_send, second_recv).wait_send()
 
     @pl.loop(1, pairs)
     def _(k):
@@ -299,8 +374,8 @@
         scratch_shapes=[
             pltpu.VMEM((own_bands, grid_rows), BF16),
             pltpu.VMEM(factor_panels.shape, F32),
-            pltpu.VMEM((chunks, bands, LANES), BF16),
-            pltpu.VMEM((bands, panel), BF16),
+            pltpu.VMEM((chunks, 2, bands // 2, LANES), BF16),
+            pltpu.VMEM((2, bands // 2, panel), BF16),
             pltpu.VMEM((own_bands, panel), F32),
             pltpu.VMEM((panel, panel), F32),
             pltpu.VMEM((panel, panel), F32),
@@ -308,19 +383,14 @@
             pltpu.VMEM((panel, panel), BF16),
             pltpu.VMEM((panel, panel), BF16),
             pltpu.VMEM((panel, panel), BF16),
-            pltpu.VMEM((chunks, LANES, panel), BF16),
-            pltpu.VMEM((chunks, LANES, panel), BF16),
+            pltpu.VMEM((rows_here // PIECE, PIECE, panel), BF16),
+            pltpu.VMEM((rows_here // PIECE, PIECE, panel), BF16),
             dma((2,)),
-            dma((chunks,)),
-            dma((chunks,)),
-            dma((chunks,)),
+            *[dma((chunks,))] * 7,
             dma((grid_count // 2,)),
             dma((grid_count,)),
             dma((grid_count // 2,)),
-            dma((chunks,)),
-            dma((chunks,)),
-            dma((chunks,)),
-            dma((chunks,)),
+            *[dma((rows_here // PIECE,))] * 4,
         ],
         compiler_params=pltpu.CompilerParams(
             collective_id=0, has_side_effects=True, vmem_limit_bytes=56 * 1024 * 1024

time: 61.2 us -> 58.9 us (0.962)
  Pallas kernels: 58.2 us -> 56.5 us
    pallas_call x1, Pallas kernels: 58.2 us -> 56.5 us  [on_device(): pl.pallas_call(functools.partial(kernel, grid_count, pt_count), out_shape...]
where the time goes in v2:
time: 58.9 us; the launch traced here: 58.7 us
  Pallas kernels  56.5 us (96%)
  local copies, waits for them, and re-layouts  2.26 us (4%)
    pallas_call x1, Pallas kernels, on_device(): pl.pallas_call(functools.partial(kernel, grid_count, pt_count), out_shape...  56.5 us
    unnamed x1, local copies, waits for them, and re-layouts  2.26 us

profile of v2, /device:TPU:24, one launch (start us, length us, event | category | flops | bytes accessed | tf_op | source)
XLA Modules:
  0.0 58.7 jit_solution(9927279195518221967)
XLA Ops:
  0.0 56.5 %shard_map.37 = f32[512,512]{1,0:T(8,128)} custom-call(s32[1,512]{1,0:T(1,128)} %bitcast.1, bf16[256,4096]{1,0:T(8,128)(2,1)} %orb.1, f32[512,1024]{1,0:T(8,128)} %fac.1), custom_call_target="tpu_custom_call" | custom-call | tf_op jit(solution)/shard_map/pallas_call | solution.py:369
  56.5 2.3 %copy.5 = f32[512,512]{1,0:T(8,128)} copy(f32[512,512]{1,0:T(8,128)} %shard_map.37) | data formatting | bytes 2097152
